TPU v7x, 32 devices: a whole 2x2x4 slice. The times are simulated.
32 devices in a mesh: seq: 2 (over x), tensor: 16 (over z, y, core).
Axes of the slice: x: 2, y: 2, z: 4, core: 2. Of those that a mesh axis runs over, the one named last changes fastest.
Arguments:
- tokens: bfloat16 [512, 4096], P(('seq', 'tensor')), may hold values from -6 to 6
- lengths: int32 [6], replicated, may hold values from 1 to 256, 512 in all
- proj_zx: bfloat16 [4096, 2, 8192], P(None, None, 'tensor'), may hold values from -0.09375 to 0.09375
- proj_bc: bfloat16 [4096, 2, 1024], P(None, None, 'tensor'), may hold values from -0.09375 to 0.09375
- proj_dt: bfloat16 [4096, 128], P(None, 'tensor'), may hold values from -0.09375 to 0.09375
- conv_x: float32 [4, 8192], P(None, 'tensor'), may hold values from -3 to 3
- conv_bc: float32 [4, 2, 1024], P(None, None, 'tensor'), may hold values from -3 to 3
- bias_x: float32 [8192], P('tensor'), may hold values from -0.5 to 0.5
- bias_bc: float32 [2, 1024], P(None, 'tensor'), may hold values from -0.5 to 0.5
- dt_bias: float32 [128], P('tensor'), may hold values from -7 to -3
- decay_rate: float32 [128], P('tensor'), may hold values from 0.02 to 1
- skip_gain: float32 [128], P('tensor'), may hold values from 0.5 to 1.5
- proj_out: bfloat16 [8192, 4096], P('tensor'), may hold values from -0.0625 to 0.0625
Outputs:
- mixed: bfloat16 [512, 4096], P(('seq', 'tensor'))
- final_states: float32 [6, 128, 64, 128], P(None, 'tensor')
Inputs may be any that keep to these rules, and one draw needn't show every extreme that they name: `lengths`: the 6 requests lie back to back in the stream in this order and fill it exactly; the longest has exactly 256 tokens.
All inputs are finite; a program needn't handle non-finite values.
Results may differ from a plain program's by a relative error of at most 0.0074.
Values may be sent and summed in bfloat16 or wider, within the bound.
A program may use at most 128 MiB of HBM per device.

v0:
```python
import jax
import jax.numpy as jnp
from jax import lax
from jax.sharding import PartitionSpec as P

GROUPS = 8


def partner_2(value, axis, bit):
    mask = 2**bit
    pairs = [(source, source ^ mask) for source in range(lax.axis_size(axis))]
    return lax.ppermute(value, axis, pairs)


def passed_along(block, axis, distance):
    devices = range(lax.axis_size(axis))
    route = [(i - distance, i) for i in devices if i - distance in devices]
    return lax.ppermute(block, axis, route)


def group_columns(bc_own, tensor_index, steps_count):
    collected = bc_own
    for bit_number in range(steps_count):
        partner = partner_2(collected, "tensor", bit_number)
        upper = tensor_index // 2**bit_number % 2
        low_first = jnp.concatenate([collected, partner], axis=2)
        high_first = jnp.concatenate([partner, collected], axis=2)
        collected = jnp.where(upper == 0, low_first, high_first)
    return collected


def body(
    tokens,
    lengths,
    proj_zx,
    proj_bc,
    proj_dt,
    conv_x,
    conv_bc,
    bias_x,
    bias_bc,
    dt_bias,
    decay_rate,
    skip_gain,
    proj_out,
):
    highest = lax.Precision.HIGHEST
    tensor_size = lax.axis_size("tensor")
    rows_dev = tokens.shape[0]
    shard_len = rows_dev * tensor_size
    seq_index = lax.axis_index("seq")
    tensor_index = lax.axis_index("tensor")
    heads_dev = decay_rate.shape[0]
    width_zx = proj_zx.shape[2]
    head_size = width_zx // heads_dev
    cols_bc = proj_bc.shape[2]
    taps_count = conv_x.shape[0]
    model_width = tokens.shape[1]
    zx_flat = proj_zx.reshape(model_width, 2 * width_zx)
    bc_flat = proj_bc.reshape(model_width, 2 * cols_bc)
    piece = lax.all_gather(tokens, "tensor", axis=0, tiled=True)
    projected = jnp.concatenate(
        [
            jnp.dot(piece, zx_flat, preferred_element_type=jnp.float32),
            jnp.dot(piece, bc_flat, preferred_element_type=jnp.float32),
            jnp.dot(piece, proj_dt, preferred_element_type=jnp.float32),
        ],
        axis=1,
    )
    gate_in = projected[:, :width_zx].astype(jnp.bfloat16)
    conv_in = projected[:, width_zx : 2 * width_zx + 2 * cols_bc].astype(jnp.bfloat16)
    step_size = jax.nn.softplus(projected[:, 2 * width_zx + 2 * cols_bc :] + dt_bias[None, :])
    row_ids = jnp.arange(shard_len, dtype=jnp.int32)
    positions = seq_index * shard_len + row_ids
    bounds = jnp.cumsum(lengths)
    reached = bounds[None, :] <= positions[:, None]
    segment = jnp.sum(reached.astype(jnp.int32), axis=1)
    seg_start = jnp.max(jnp.where(reached, bounds[None, :], 0), axis=1)
    edge_rows = conv_in[shard_len - (taps_count - 1) :]
    before = passed_along(edge_rows, "seq", 1)
    extended = jnp.concatenate([before, conv_in], axis=0)
    conv_taps = jnp.concatenate([conv_x, conv_bc.reshape(taps_count, 2 * cols_bc)], axis=1)
    conv_offset = jnp.concatenate([bias_x, bias_bc.reshape(2 * cols_bc)])
    convolved = jnp.zeros((shard_len, conv_taps.shape[1]), jnp.float32) + conv_offset[None, :]
    for lag_index in range(taps_count):
        lagged = extended[
            taps_count - 1 - lag_index : taps_count - 1 - lag_index + shard_len
        ].astype(jnp.float32)
        keep_mask = (positions - lag_index >= seg_start).astype(jnp.float32)
        convolved = convolved + conv_taps[lag_index][None, :] * lagged * keep_mask[:, None]
    activated = jax.nn.silu(convolved).astype(jnp.bfloat16)
    x_conv = activated[:, :width_zx]
    bc_own = activated[:, width_zx:].reshape(shard_len, 2, cols_bc)
    per_group = tensor_size // GROUPS
    steps_count = per_group.bit_length() - 1
    bc_group = group_columns(bc_own, tensor_index, steps_count).astype(jnp.float32)
    state_in_proj = bc_group[:, 0]
    state_out_proj = bc_group[:, 1]
    x_float = x_conv.astype(jnp.float32).reshape(shard_len, heads_dev, head_size)
    log_decay = -decay_rate[None, :] * step_size
    cumulative = jnp.cumsum(log_decay, axis=0)
    cumulative_t = cumulative.T
    valid = (segment[:, None] == segment[None, :]) & (row_ids[:, None] >= row_ids[None, :])
    spread = cumulative_t[:, :, None] - cumulative_t[:, None, :]
    decay_matrix = jnp.where(valid[None], jnp.exp(jnp.where(valid[None], spread, 0.0)), 0.0)
    scores = jnp.dot(state_out_proj, state_in_proj.T, precision=highest)
    mixing = decay_matrix * scores[None] * step_size.T[:, None, :]
    y_local = jnp.einsum("hts,shp->thp", mixing, x_float, precision=highest)
    before_pos = seq_index * shard_len - 1
    seg_before = jnp.sum((bounds <= before_pos).astype(jnp.int32))
    carried = (segment == seg_before).astype(jnp.float32)
    entry_gain = jnp.exp(cumulative) * carried[:, None]
    n_seg = lengths.shape[0]
    end_rows = bounds - 1 - seq_index * shard_len
    inside = (end_rows >= 0) & (end_rows < shard_len)
    target_rows = jnp.concatenate([end_rows, jnp.full((1,), shard_len - 1, jnp.int32)])
    target_seg = jnp.concatenate([jnp.arange(n_seg, dtype=jnp.int32), segment[shard_len - 1 :]])
    target_ok = jnp.concatenate([inside, jnp.ones((1,), bool)])
    picker = (row_ids[None, :] == target_rows[:, None]).astype(jnp.float32)
    cum_end = jnp.dot(picker, cumulative, precision=highest)
    reach = (
        target_ok[:, None]
        & (row_ids[None, :] <= target_rows[:, None])
        & (segment[None, :] == target_seg[:, None])
    )
    gap_end = cum_end[:, :, None] - cumulative_t[None, :, :]
    end_weight = (
        jnp.where(reach[:, None, :], jnp.exp(jnp.where(reach[:, None, :], gap_end, 0.0)), 0.0)
        * step_size.T[None]
    )
    states = jnp.einsum("khs,shp,sn->khpn", end_weight, x_float, state_in_proj, precision=highest)
    end_local = states[:n_seg]
    shard_state = states[n_seg]
    end_gain = jnp.where((target_ok & (target_seg == seg_before))[:, None], jnp.exp(cum_end), 0.0)
    shard_gain = end_gain[n_seg]
    end_gain_seg = end_gain[:n_seg]
    gathered = (
        lax.all_gather(shard_gain[None], "seq", axis=0, tiled=True),
        lax.all_gather(shard_state[None], "seq", axis=0, tiled=True),
        lax.all_gather(end_gain_seg[None], "seq", axis=0, tiled=True),
        lax.all_gather(end_local[None], "seq", axis=0, tiled=True),
    )
    gains_all, states_all, egains_all, elocal_all = gathered

    def fold_step(carry, item):
        gain_now, state_now = item
        return (gain_now[:, None, None] * carry + state_now, carry)

    last_state, incoming = lax.scan(
        fold_step, jnp.zeros(shard_state.shape, jnp.float32), (gains_all, states_all)
    )
    state_entry = lax.dynamic_index_in_dim(incoming, seq_index, 0, keepdims=False)
    final_states = jnp.sum(elocal_all + egains_all[:, :, :, None, None] * incoming[:, None], axis=0)
    y_entry = (
        jnp.einsum("tn,hpn->thp", state_out_proj, state_entry, precision=highest)
        * entry_gain[:, :, None]
    )
    y_total = y_local + y_entry + skip_gain[None, :, None] * x_float
    gate_values = jax.nn.silu(gate_in.astype(jnp.float32)).reshape(shard_len, heads_dev, head_size)
    gated = (y_total * gate_values).reshape(shard_len, width_zx).astype(jnp.bfloat16)
    mixed = lax.psum_scatter(
        jnp.dot(gated, proj_out, preferred_element_type=jnp.float32),
        "tensor",
        scatter_dimension=0,
        tiled=True,
    )
    return (mixed.astype(jnp.bfloat16), final_states)


def solution(mesh):
    in_specs = (
        P(("seq", "tensor"), None),
        P(),
        P(None, None, "tensor"),
        P(None, None, "tensor"),
        P(None, "tensor"),
        P(None, "tensor"),
        P(None, None, "tensor"),
        P("tensor"),
        P(None, "tensor"),
        P("tensor"),
        P("tensor"),
        P("tensor"),
        P("tensor", None),
    )
    out_specs = (P(("seq", "tensor"), None), P(None, "tensor", None, None))
    return jax.shard_map(body, mesh=mesh, in_specs=in_specs, out_specs=out_specs, check_vma=False)
```

profile of v0, /device:TPU:0, one launch (start us, length us, event | category | flops | bytes accessed | tf_op | source)
XLA Modules:
  0.0 207.5 jit_solution(12037769887396977083)
XLA Ops:
  8.1 9.3 %copy.64 = bf16[512,8,2,512]{3,1,2,0:T(8,128)(2,1)} copy(bf16[512,8,2,512]{3,2,1,0:T(2,128)(2,1)} %bitcast.74) | data formatting | bytes 16777216
  19.2 1.4 compare_and_fusion
  21.4 32.9 %all-gather.7.cloned.1.call-done = bf16[256,4096]{1,0:T(8,128)(2,1)} async-done(((bf16[16,4096]{1,0:T(8,128)(2,1)}), bf16[256,4096]{1,0:T(8,128)(2,1)}) %all-gather.7.cloned.1.call-update) | async-done | bytes 2097168 | tf_op jit(solution)/shard_map/all_gather | solution.py:61
  54.3 6.5 %convolution_convert_fusion = bf16[256,1024]{1,0:T(8,128)(2,1)S(1)} fusion(bf16[256,4096]{1,0:T(8,128)(2,1)} %all-gather.7.cloned.1.call-done, bf16[4096,1024]{1,0:T(8,128)(2,1)} %bitcast.75), kind=kOutput, calls=%fused_computation.17 | convolution fusion | flops 2147745792 | bytes 11010048 | tf_op jit(solution)/shard_map/dot_general | solution.py:64
  61.7 3.4 %collective-permute-start = (bf16[3,640]{1,0:T(4,128)(2,1)S(1)}, bf16[3,640]{1,0:T(4,128)(2,1)S(1)}, u32[]{:S(2)}, u32[]{:S(2)}) collective-permute-start(bf16[3,640]{1,0:T(4,128)(2,1)S(1)} %pad_maximum_fusion.1), channel_id=1, source_target_pairs={{0,16},{1,17},{2,18},{3,19},{4,20},{5,21},{6,22},{7,23},{8,24},{9,... | collective-permute-start | bytes 11528 | tf_op jit(solution)/shard_map/ppermute | solution.py:18
  66.7 0.8 exponential_select_fusion
  70.0 2.7 %fusion.12 = f32[7,8,64,128]{3,2,0,1:T(8,128)S(1)} fusion(f32[256,8,7]{0,2,1:T(8,128)} %multiply_bitcast_fusion, f32[256,8,64]{0,2,1:T(8,128)S(1)} %convert.14, bf16[256,2,128]{2,0,1:T(8,128)(2,1)S(1)} %maximum_select_fusion), kind=kOutput, calls=%fused_computation.16 | convolution fusion | flops 1410203648 | bytes 2482176 | tf_op jit(solution)/shard_map/khs,shp,sn->khpn/dot_general | solution.py:131
  72.7 1.2 slice.104
  74.0 1.4 fusion.36
  75.5 1.2 slice_bitcast_fusion.1
  76.6 4.6 %all-gather.2 = f32[2,1,8]{2,1,0:T(1,128)} all-gather(f32[1,1,8]{2,1,0:T(1,128)} %slice_bitcast_fusion.1), channel_id=1, replica_groups=mesh['seq'=2,'tensor'=16] {'seq'}, dimensions={0}, use_global_device_ids=true | all-gather | bytes 96 | tf_op jit(solution)/shard_map/all_gather | solution.py:138
  81.2 1.9 convert_multiply_fusion
  83.2 2.1 copy.57
  85.3 15.0 %all_gather.17 = f32[2,8,64,128]{3,2,0,1:T(8,128)S(1)} all-gather(f32[1,8,64,128]{3,2,0,1:T(8,128)S(1)} %slice.102), channel_id=1, replica_groups=mesh['seq'=2,'tensor'=16] {'seq'}, dimensions={0}, use_global_device_ids=true | all-gather | bytes 786432 | tf_op jit(solution)/shard_map/all_gather | solution.py:139
  100.4 3.5 %fusion.15 = f32[256,8,64]{0,2,1:T(8,128)} fusion(bf16[256,8,64]{0,2,1:T(8,128)(2,1)S(1)} %bitcast.78, f32[8,256]{1,0:T(8,128)S(1)} %compare_select_fusion, f32[256,256]{1,0:T(8,128)S(1)} %fusion.39, f32[8,256]{1,0:T(8,128)} %copy-done.6, pred[256,256]{1,0:T(8,128)(4,1)} %fusion.36), kind=kOutput, calls=%fused_computation.18 | convolution fusion | flops 405274624 | bytes 1130496 | tf_op jit(solution)/shard_map/hts,shp->thp/dot_general | solution.py:108
  104.0 1.6 while.13
  105.6 1.4 fusion.21
  107.0 5.4 %fusion.55 = f32[256,4096]{1,0:T(8,128)} fusion(bf16[256,512]{0,1:T(8,128)(2,1)S(1)} %bitcast.81, bf16[512,4096]{1,0:T(8,128)(2,1)} %param.27), kind=kOutput, calls=%fused_computation.103 | convolution fusion | flops 1073741824 | bytes 8650752 | tf_op jit(solution)/shard_map/dot_general | solution.py:162
  113.1 4.4 %all-gather.3 = f32[2,6,8]{2,1,0:T(8,128)S(1)} all-gather(f32[1,6,8]{2,1,0:T(8,128)S(1)} %slice_bitcast_fusion), channel_id=3, replica_groups=mesh['seq'=2,'tensor'=16] {'seq'}, dimensions={0}, use_global_device_ids=true | all-gather | bytes 576 | tf_op jit(solution)/shard_map/all_gather | solution.py:140
  117.6 5.5 %all-gather.9.cloned.1.call-done = f32[12,8,64,128]{3,2,0,1:T(8,128)} async-done(((f32[6,8,64,128]{3,2,0,1:T(8,128)}), f32[12,8,64,128]{3,2,0,1:T(8,128)}) %all-gather.9.cloned.1.call-update) | async-done | bytes 3145744 | tf_op jit(solution)/shard_map/all_gather | solution.py:141
  123.1 2.5 %add_reduce_fusion = f32[6,8,64,128]{3,2,0,1:T(8,128)S(1)} fusion(f32[2,6,8,64,128]{4,3,1,0,2:T(8,128)} %bitcast.76, f32[2,6,8]{1,0,2:T(2,128)S(1)} %copy.58, f32[2,8,64,128]{3,2,1,0:T(8,128)S(1)} %get-tuple-element.29), kind=kLoop, calls=%fused_computation.6 | loop fusion | flops 1966080 | bytes 5243264 | tf_op jit(solution)/shard_map/reduce_sum | solution.py:153
  125.6 1.3 copy.60
  127.0 72.4 %reduce-scatter.2.cloned.1.call-done = f32[16,4096]{1,0:T(8,128)} async-done(((f32[256,4096]{1,0:T(8,128)}), f32[16,4096]{1,0:T(8,128)}) %reduce-scatter.2.cloned.1.call-update) | async-done | bytes 262160 | tf_op jit(solution)/shard_map/reduce_scatter | solution.py:161
  199.4 1.6 convert_element_type.88
  (93 shorter events, 10.8 us)
Async XLA Ops:
  7.2 53.6 %copy-start = (bf16[4096,2,64]{0,2,1:T(8,128)(2,1)S(1)}, bf16[4096,2,64]{0,2,1:T(8,128)(2,1)}, u32[]{:S(2)}) copy-start(bf16[4096,2,64]{0,2,1:T(8,128)(2,1)} %param.18) | copy-start | bytes 3145732
  7.2 47.1 %all-gather.7.cloned.1.call-start = ((), (), s32[]{:S(2)}) async-start(), calls=%async_computation.1 | async-start | bytes 2228224 | tf_op jit(solution)/shard_map/all_gather | solution.py:61
  7.9 115.2 %all-gather.9.cloned.1.call-start = ((), (), s32[]{:S(2)}) async-start(), calls=%async_computation.3 | async-start | bytes 4718592 | tf_op jit(solution)/shard_map/all_gather | solution.py:141
  8.0 9.4 %copy-start.15 = (s32[6]{0:T(128)S(1)}, s32[6]{0:T(128)}, u32[]{:S(2)}) copy-start(s32[6]{0:T(128)} %param.16) | copy-start | bytes 76
  8.0 9.6 %copy-start.9 = (f32[4,2,64]{2,1,0:T(2,128)S(1)}, f32[4,2,64]{2,1,0:T(2,128)}, u32[]{:S(2)}) copy-start(f32[4,2,64]{2,1,0:T(2,128)} %param.21) | copy-start | bytes 6148
  8.0 9.7 %copy-start.14 = (f32[2,64]{1,0:T(2,128)S(1)}, f32[2,64]{1,0:T(2,128)}, u32[]{:S(2)}) copy-start(f32[2,64]{1,0:T(2,128)} %param.23) | copy-start | bytes 1540
  8.0 9.7 %copy-start.16 = (f32[8]{0:T(128)S(1)}, f32[8]{0:T(128)}, u32[]{:S(2)}) copy-start(f32[8]{0:T(128)} %param.25) | copy-start | bytes 100
  8.0 12.5 %copy-start.8 = (f32[4,512]{1,0:T(4,128)S(1)}, f32[4,512]{1,0:T(4,128)}, u32[]{:S(2)}) copy-start(f32[4,512]{1,0:T(4,128)} %param.20) | copy-start | bytes 24580
  8.1 12.5 %copy-start.11 = (f32[512]{0:T(512)S(1)}, f32[512]{0:T(512)}, u32[]{:S(2)}) copy-start(f32[512]{0:T(512)} %param.22) | copy-start | bytes 6148
  17.9 3.4 %copy-start.7 = (s32[256]{0:T(256)}, s32[256]{0:T(256)S(1)}, u32[]{:S(2)}) copy-start(s32[256]{0:T(256)S(1)} %get-tuple-element.76) | copy-start | bytes 3076
  54.3 6.5 %copy-start.1 = (bf16[256,4096]{1,0:T(8,128)(2,1)S(1)}, bf16[256,4096]{1,0:T(8,128)(2,1)}, u32[]{:S(2)}) copy-start(bf16[256,4096]{1,0:T(8,128)(2,1)} %all-gather.7.cloned.1.call-done) | copy-start | bytes 6291460
  60.8 6.7 %copy-start.2 = (bf16[256,1024]{1,0:T(8,128)(2,1)}, bf16[256,1024]{1,0:T(8,128)(2,1)S(1)}, u32[]{:S(2)}) copy-start(bf16[256,1024]{1,0:T(8,128)(2,1)S(1)} %convolution_convert_fusion) | copy-start | bytes 1572868
  60.8 4.2 %copy-start.5 = (bf16[4096,8]{0,1:T(8,128)(2,1)S(1)}, bf16[4096,8]{0,1:T(8,128)(2,1)}, u32[]{:S(2)}) copy-start(bf16[4096,8]{0,1:T(8,128)(2,1)} %param.19) | copy-start | bytes 196612
  60.8 4.2 %copy-start.12 = (f32[8]{0:T(128)S(1)}, f32[8]{0:T(128)}, u32[]{:S(2)}) copy-start(f32[8]{0:T(128)} %param.24) | copy-start | bytes 100
  61.7 5.9 %collective-permute-start = (bf16[3,640]{1,0:T(4,128)(2,1)S(1)}, bf16[3,640]{1,0:T(4,128)(2,1)S(1)}, u32[]{:S(2)}, u32[]{:S(2)}) collective-permute-start(bf16[3,640]{1,0:T(4,128)(2,1)S(1)} %pad_maximum_fusion.1), channel_id=1, source_target_pairs={{0,16},{1,17},{2,18},{3,19},{4,20},{5,21},{6,22},{7,23},{8,24},{9,... | collective-permute-start | bytes 11528 | tf_op jit(solution)/shard_map/ppermute | solution.py:18
  66.7 3.2 %copy-start.6 = (f32[8,256]{1,0:T(8,128)}, f32[8,256]{1,0:T(8,128)S(1)}, u32[]{:S(2)}) copy-start(f32[8,256]{1,0:T(8,128)S(1)} %get-tuple-element.93) | copy-start | bytes 24580
  68.5 1.4 collective-permute-start.1
  74.0 125.4 %reduce-scatter.2.cloned.1.call-start = ((), (), s32[]{:S(2)}) async-start(), calls=%async_computation.2 | async-start | bytes 4456448 | tf_op jit(solution)/shard_map/reduce_scatter | solution.py:161
  100.4 3.5 %copy-start.4 = (f32[2,8,64,128]{3,2,1,0:T(8,128)S(1)}, f32[2,8,64,128]{3,2,1,0:T(8,128)}, u32[]{:S(2)}) copy-start(f32[2,8,64,128]{3,2,1,0:T(8,128)} %custom-call.2) | copy-start | bytes 1572868
  104.0 1.6 copy-start.3
  104.0 1.6 copy-start.13
  112.4 0.7 copy-start.10
Sparse Core Ops, SparseCore 0:
  10.2 44.0 all-gather.6
  74.1 48.9 all-gather.8
  127.0 72.3 reduce-scatter.1
where the time goes:
time: 208 us
  waiting for transfers between devices  112 us (54%)
  blocking collectives  24 us (12%)
  matrix products  22 us (11%)
  local copies, waits for them, and re-layouts  18.7 us (9%)
  between operations  14.1 us (7%)
  other arithmetic  13.1 us (6%)
  starting transfers between devices  3.56 us (2%)
    reduce_scatter x1, waiting for transfers between devices, body(): lax.psum_scatter(jnp.dot(gated, proj_out, preferred_element_type=jnp.floa...  72.4 us
    all_gather x1, waiting for transfers between devices, body(): piece = lax.all_gather(tokens, 'tensor', axis=0, tiled=True)  32.9 us
    all_gather x1, blocking collectives, body(): lax.all_gather(shard_state[None], 'seq', axis=0, tiled=True)  15 us
    unnamed x39, local copies, waits for them, and re-layouts  12.6 us
    dot_general x1, matrix products, body(): jnp.dot(piece, zx_flat, preferred_element_type=jnp.float32)  6.49 us
    all_gather x1, waiting for transfers between devices, body(): lax.all_gather(end_local[None], 'seq', axis=0, tiled=True)  5.54 us
    dot_general x1, matrix products, body(): jnp.dot(gated, proj_out, preferred_element_type=jnp.float32)  5.4 us
    all_gather x1, blocking collectives, body(): lax.all_gather(shard_gain[None], 'seq', axis=0, tiled=True)  4.62 us
  transfers between devices with their start and end apart: 5, of which 4 were waited for; matrix products, arithmetic and copies ran while one was open for 19% of the time, Pallas kernels for 0%

commit v1 on v0

--- a/solution.py
+++ b/solution.py
@@ -4,6 +4,18 @@
 from jax.sharding import PartitionSpec as P
 
 GROUPS = 8
+
+
+def collect(array, axis, dim):
+    ways, here, step = (lax.axis_size(axis), lax.axis_index(axis), array.shape[dim])
+    line, have = (array, 1)
+    while have < ways:
+        line = jnp.concatenate(
+            [line, lax.ppermute(line, axis, [(d, (d - have) % ways) for d in range(ways)])],
+            axis=dim,
+        )
+        have = 2 * have
+    return jnp.roll(line, here * step, axis=dim)
 
 
 def partner_2(value, axis, bit):
@@ -138,7 +150,7 @@
         lax.all_gather(shard_gain[None], "seq", axis=0, tiled=True),
         lax.all_gather(shard_state[None], "seq", axis=0, tiled=True),
         lax.all_gather(end_gain_seg[None], "seq", axis=0, tiled=True),
-        lax.all_gather(end_local[None], "seq", axis=0, tiled=True),
+        collect(end_local[None], "seq", 0),
     )
     gains_all, states_all, egains_all, elocal_all = gathered
 

time: 208 us -> 180 us (0.87)
  waiting for transfers between devices: 112 us -> 63.2 us
  blocking collectives: 24 us -> 47.2 us
  matrix products: 22 us -> 19.4 us
  local copies, waits for them, and re-layouts: 18.7 us -> 16.5 us
    reduce_scatter x1, waiting for transfers between devices: 72.4 us -> 30.3 us  [body(): lax.psum_scatter(jnp.dot(gated, proj_out, preferred_element_type=jnp.floa...]
    all_gather x1, blocking collectives: 4.38 us -> 34.3 us  [body(): lax.all_gather(end_gain_seg[None], 'seq', axis=0, tiled=True)]
    all_gather x1, blocking collectives: 15 us -> 8.67 us  [body(): lax.all_gather(shard_state[None], 'seq', axis=0, tiled=True)]
    all_gather x1 -> x0, waiting for transfers between devices: 5.54 us -> none  [body(): lax.all_gather(end_local[None], 'seq', axis=0, tiled=True)]
    dot_general x1, matrix products: 5.4 us -> 3.24 us  [body(): jnp.dot(gated, proj_out, preferred_element_type=jnp.float32)]
    unnamed x39 -> x35, local copies, waits for them, and re-layouts: 12.6 us -> 11.4 us
  transfers between devices with their start and end apart: 5 -> 5, of which waited for: 4 -> 2; matrix products, arithmetic and copies ran while one was open for 19% -> 13% of each run, Pallas kernels for 0% -> 0%
where the time goes in v1:
time: 180 us; the launch traced here: 179 us
  waiting for transfers between devices  63.2 us (35%)
  blocking collectives  47.2 us (26%)
  matrix products  19.4 us (11%)
  local copies, waits for them, and re-layouts  16.5 us (9%)
  between operations  14.4 us (8%)
  other arithmetic  14.1 us (8%)
  starting transfers between devices  4.42 us (2%)
    all_gather x1, blocking collectives, body(): lax.all_gather(end_gain_seg[None], 'seq', axis=0, tiled=True)  34.3 us
    all_gather x1, waiting for transfers between devices, body(): piece = lax.all_gather(tokens, 'tensor', axis=0, tiled=True)  32.2 us
    reduce_scatter x1, waiting for transfers between devices, body(): lax.psum_scatter(jnp.dot(gated, proj_out, preferred_element_type=jnp.floa...  30.3 us
    unnamed x35, local copies, waits for them, and re-layouts  11.4 us
    all_gather x1, blocking collectives, body(): lax.all_gather(shard_state[None], 'seq', axis=0, tiled=True)  8.67 us
    dot_general x1, matrix products, body(): jnp.dot(piece, zx_flat, preferred_element_type=jnp.float32)  6.49 us
    all_gather x1, blocking collectives, body(): lax.all_gather(shard_gain[None], 'seq', axis=0, tiled=True)  4.16 us
  transfers between devices with their start and end apart: 5, of which 2 were waited for; matrix products, arithmetic and copies ran while one was open for 13% of the time, Pallas kernels for 0%

profile of v1, /device:TPU:0, one launch (start us, length us, event | category | flops | bytes accessed | tf_op | source)
XLA Modules:
  0.0 179.1 jit_solution(15415721590930744377)
XLA Ops:
  8.1 9.3 %copy.60 = bf16[512,8,2,512]{3,1,2,0:T(8,128)(2,1)} copy(bf16[512,8,2,512]{3,2,1,0:T(2,128)(2,1)} %bitcast.75) | data formatting | bytes 16777216
  19.2 1.4 compare_and_fusion
  22.1 32.2 %all-gather.5.cloned.1.call-done = bf16[256,4096]{1,0:T(8,128)(2,1)} async-done(((bf16[16,4096]{1,0:T(8,128)(2,1)}), bf16[256,4096]{1,0:T(8,128)(2,1)}) %all-gather.5.cloned.1.call-update) | async-done | bytes 2097168 | tf_op jit(solution)/shard_map/all_gather | solution.py:73
  54.3 6.5 %convolution_convert_fusion = bf16[256,1024]{1,0:T(8,128)(2,1)S(1)} fusion(bf16[256,4096]{1,0:T(8,128)(2,1)} %all-gather.5.cloned.1.call-done, bf16[4096,1024]{1,0:T(8,128)(2,1)} %bitcast.76), kind=kOutput, calls=%fused_computation.26 | convolution fusion | flops 2147745792 | bytes 11010048 | tf_op jit(solution)/shard_map/dot_general | solution.py:76
  61.0 0.8 convolution_convert_fusion.1
  61.8 3.4 %collective-permute-start = (bf16[3,640]{1,0:T(4,128)(2,1)S(1)}, bf16[3,640]{1,0:T(4,128)(2,1)S(1)}, u32[]{:S(2)}, u32[]{:S(2)}) collective-permute-start(bf16[3,640]{1,0:T(4,128)(2,1)S(1)} %pad_maximum_fusion.1), channel_id=1, source_target_pairs={{0,16},{1,17},{2,18},{3,19},{4,20},{5,21},{6,22},{7,23},{8,24},{9,... | collective-permute-start | bytes 11528 | tf_op jit(solution)/shard_map/ppermute | solution.py:30
  69.4 4.2 %all-gather.1 = f32[2,1,8]{2,1,0:T(1,128)} all-gather(f32[1,1,8]{2,1,0:T(1,128)S(1)} %slice_bitcast_fusion.2), channel_id=1, replica_groups=mesh['seq'=2,'tensor'=16] {'seq'}, dimensions={0}, use_global_device_ids=true | all-gather | bytes 96 | tf_op jit(solution)/shard_map/all_gather | solution.py:150
  73.5 1.0 copy.54
  74.9 0.9 fusion.44
  75.8 2.7 %fusion.17 = f32[7,8,64,128]{3,2,0,1:T(8,128)S(1)} fusion(f32[256,8,7]{0,2,1:T(8,128)} %multiply_bitcast_fusion, f32[256,8,64]{0,2,1:T(8,128)S(1)} %convert.14, bf16[256,2,128]{2,0,1:T(8,128)(2,1)S(1)} %maximum_select_fusion), kind=kOutput, calls=%fused_computation.25 | convolution fusion | flops 1410203648 | bytes 2482176 | tf_op jit(solution)/shard_map/khs,shp,sn->khpn/dot_general | solution.py:143
  78.5 8.7 %all_gather.14 = f32[2,8,64,128]{3,2,0,1:T(8,128)} all-gather(f32[1,8,64,128]{3,2,0,1:T(8,128)S(1)} %slice.102), channel_id=1, replica_groups=mesh['seq'=2,'tensor'=16] {'seq'}, dimensions={0}, use_global_device_ids=true | all-gather | bytes 786432 | tf_op jit(solution)/shard_map/all_gather | solution.py:151
  87.2 4.9 %while.13 = (s32[]{:T(128)}, f32[8,64,128]{2,1,0:T(8,128)S(1)}, f32[2,8,64,128]{3,2,1,0:T(8,128)}, f32[2,8]{1,0:T(2,128)}, f32[2,8,64,128]{3,2,0,1:T(8,128)}, /*index=5*/s32[]{:T(128)}, s32[]{:T(128)}) while((s32[]{:T(128)}, f32[8,64,128]{2,1,0:T(8,128)S(1)}, f32[2,8,64,128]{3,2,1,0:T(8,128)}, f32[2,8]{1,0:T(2,128)}, ...), condition=%wide.region_7.8_spmd.clone, body=%wide.region_6.7_spmd.clone.sunk | while | flops 262147 | bytes 1310924 | solution.py:161
  88.6 1.0 bitcast_add_fusion.2
  91.1 1.0 bitcast_add_fusion.2
  92.1 2.9 %fusion.20 = f32[256,8,64]{0,2,1:T(8,128)S(1)} fusion(bf16[256,8,64]{0,2,1:T(8,128)(2,1)S(1)} %bitcast.78, f32[8,256]{1,0:T(8,128)S(1)} %compare_select_fusion, f32[256,256]{1,0:T(8,128)} %fusion.44, f32[8,256]{1,0:T(8,128)} %copy-done.4, pred[256,256]{1,0:T(8,128)(4,1)} %fusion.41), kind=kOutput, calls=%fused_computation.27 | convolution fusion | flops 405274624 | bytes 1130496 | tf_op jit(solution)/shard_map/hts,shp->thp/dot_general | solution.py:120
  95.1 1.5 fusion.26
  96.6 3.2 %fusion.60 = f32[256,4096]{1,0:T(8,128)} fusion(bf16[256,512]{0,1:T(8,128)(2,1)S(1)} %bitcast.81, bf16[512,4096]{1,0:T(8,128)(2,1)S(1)} %copy-done.1), kind=kOutput, calls=%fused_computation.112 | convolution fusion | flops 1073741824 | bytes 8650752 | tf_op jit(solution)/shard_map/dot_general | solution.py:174
  99.9 1.2 slice_bitcast_fusion
  101.1 0.9 collective-permute-start.2
  102.0 34.3 %all-gather.2 = f32[2,6,8]{2,1,0:T(8,128)S(1)} all-gather(f32[1,6,8]{2,1,0:T(8,128)S(1)} %slice_bitcast_fusion.1), channel_id=2, replica_groups=mesh['seq'=2,'tensor'=16] {'seq'}, dimensions={0}, use_global_device_ids=true | all-gather | bytes 576 | tf_op jit(solution)/shard_map/all_gather | solution.py:152
  136.4 2.6 %fusion.7 = f32[6,8,64,128]{3,2,0,1:T(8,128)S(1)} fusion(s32[]{:T(128)S(6)} %select_n.73, f32[1,6,8,64,128]{4,3,1,2,0:T(8,128)} %slice_bitcast_fusion, f32[1,6,8,64,128]{4,3,1,2,0:T(8,128)S(1)} %collective-permute-done.2, f32[2,6,8]{1,2,0:T(8,128)S(1)} %copy.55, f32[2,8,64,128]{3,2,1,0:T(8,128)} %get-tuple-element.29), kind=kLoop, calls=%fused_computation.14 | loop fusion | flops 4325376 | bytes 5243268 | tf_op jit(solution)/shard_map/reduce_sum | solution.py:165
  139.1 1.3 copy.56
  140.4 30.3 %reduce-scatter.2.cloned.1.call-done = f32[16,4096]{1,0:T(8,128)} async-done(((f32[256,4096]{1,0:T(8,128)}), f32[16,4096]{1,0:T(8,128)}) %reduce-scatter.2.cloned.1.call-update) | async-done | bytes 262160 | tf_op jit(solution)/shard_map/reduce_scatter | solution.py:173
  170.7 1.6 convert_element_type.88
  (88 shorter events, 11.7 us)
Async XLA Ops:
  7.2 53.8 %copy-start = (bf16[4096,2,64]{0,2,1:T(8,128)(2,1)S(1)}, bf16[4096,2,64]{0,2,1:T(8,128)(2,1)}, u32[]{:S(2)}) copy-start(bf16[4096,2,64]{0,2,1:T(8,128)(2,1)} %param.18) | copy-start | bytes 3145732
  7.2 47.1 %all-gather.5.cloned.1.call-start = ((), (), s32[]{:S(2)}) async-start(), calls=%async_computation.1 | async-start | bytes 2228224 | tf_op jit(solution)/shard_map/all_gather | solution.py:73
  7.9 162.8 %reduce-scatter.2.cloned.1.call-start = ((), (), s32[]{:S(2)}) async-start(), calls=%async_computation.2 | async-start | bytes 4456448 | tf_op jit(solution)/shard_map/reduce_scatter | solution.py:173
  8.0 9.4 %copy-start.13 = (s32[6]{0:T(128)S(1)}, s32[6]{0:T(128)}, u32[]{:S(2)}) copy-start(s32[6]{0:T(128)} %param.16) | copy-start | bytes 76
  8.0 9.6 %copy-start.6 = (f32[4,2,64]{2,1,0:T(2,128)S(1)}, f32[4,2,64]{2,1,0:T(2,128)}, u32[]{:S(2)}) copy-start(f32[4,2,64]{2,1,0:T(2,128)} %param.21) | copy-start | bytes 6148
  8.0 9.7 %copy-start.12 = (f32[2,64]{1,0:T(2,128)S(1)}, f32[2,64]{1,0:T(2,128)}, u32[]{:S(2)}) copy-start(f32[2,64]{1,0:T(2,128)} %param.23) | copy-start | bytes 1540
  8.0 9.7 %copy-start.14 = (f32[8]{0:T(128)S(1)}, f32[8]{0:T(128)}, u32[]{:S(2)}) copy-start(f32[8]{0:T(128)} %param.25) | copy-start | bytes 100
  8.0 12.5 %copy-start.5 = (f32[4,512]{1,0:T(4,128)S(1)}, f32[4,512]{1,0:T(4,128)}, u32[]{:S(2)}) copy-start(f32[4,512]{1,0:T(4,128)} %param.20) | copy-start | bytes 24580
  8.1 12.5 %copy-start.9 = (f32[512]{0:T(512)S(1)}, f32[512]{0:T(512)}, u32[]{:S(2)}) copy-start(f32[512]{0:T(512)} %param.22) | copy-start | bytes 6148
  54.3 6.7 %copy-start.2 = (bf16[256,4096]{1,0:T(8,128)(2,1)S(1)}, bf16[256,4096]{1,0:T(8,128)(2,1)}, u32[]{:S(2)}) copy-start(bf16[256,4096]{1,0:T(8,128)(2,1)} %all-gather.5.cloned.1.call-done) | copy-start | bytes 6291460
  61.0 4.2 %copy-start.3 = (bf16[4096,8]{0,1:T(8,128)(2,1)S(1)}, bf16[4096,8]{0,1:T(8,128)(2,1)}, u32[]{:S(2)}) copy-start(bf16[4096,8]{0,1:T(8,128)(2,1)} %param.19) | copy-start | bytes 196612
  61.0 4.2 %copy-start.10 = (f32[8]{0:T(128)S(1)}, f32[8]{0:T(128)}, u32[]{:S(2)}) copy-start(f32[8]{0:T(128)} %param.24) | copy-start | bytes 100
  61.8 5.9 %collective-permute-start = (bf16[3,640]{1,0:T(4,128)(2,1)S(1)}, bf16[3,640]{1,0:T(4,128)(2,1)S(1)}, u32[]{:S(2)}, u32[]{:S(2)}) collective-permute-start(bf16[3,640]{1,0:T(4,128)(2,1)S(1)} %pad_maximum_fusion.1), channel_id=1, source_target_pairs={{0,16},{1,17},{2,18},{3,19},{4,20},{5,21},{6,22},{7,23},{8,24},{9,... | collective-permute-start | bytes 11528 | tf_op jit(solution)/shard_map/ppermute | solution.py:30
  66.8 7.9 %copy-start.4 = (f32[8,256]{1,0:T(8,128)}, f32[8,256]{1,0:T(8,128)S(1)}, u32[]{:S(2)}) copy-start(f32[8,256]{1,0:T(8,128)S(1)} %get-tuple-element.93) | copy-start | bytes 24580
  67.0 0.6 copy-start.7
  68.6 6.2 %collective-permute-start.1 = (bf16[256,2,64]{2,0,1:T(8,128)(2,1)S(1)}, bf16[256,2,64]{2,0,1:T(8,128)(2,1)S(1)}, u32[]{:S(2)}, u32[]{:S(2)}) collective-permute-start(bf16[256,2,64]{2,0,1:T(8,128)(2,1)S(1)} %copy.50), channel_id=1, source_target_pairs={{0,1},{1,0},{2,3},{3,2},{4,5},{5,4},{6,7},{7,6},{8,9},{9,8},{10,11... | collective-permute-start | bytes 196616 | tf_op jit(solution)/shard_map/ppermute | solution.py:24
  92.1 2.9 %copy-start.11 = (f32[8]{0:T(128)S(1)}, f32[8]{0:T(128)}, u32[]{:S(2)}) copy-start(f32[8]{0:T(128)} %param.26) | copy-start | bytes 100
  92.1 4.5 %copy-start.1 = (bf16[512,4096]{1,0:T(8,128)(2,1)S(1)}, bf16[512,4096]{1,0:T(8,128)(2,1)}, u32[]{:S(2)}) copy-start(bf16[512,4096]{1,0:T(8,128)(2,1)} %param.27) | copy-start | bytes 12582916
  99.9 2.2 %copy-start.8 = (f32[7,8]{1,0:T(8,128)S(1)}, f32[7,8]{1,0:T(8,128)}, u32[]{:S(2)}) copy-start(f32[7,8]{1,0:T(8,128)} %copy-done.7) | copy-start | bytes 676
  101.1 35.3 %collective-permute-start.2 = (f32[1,6,8,64,128]{4,3,1,2,0:T(8,128)}, f32[1,6,8,64,128]{4,3,1,2,0:T(8,128)S(1)}, u32[]{:S(2)}, u32[]{:S(2)}) collective-permute-start(f32[1,6,8,64,128]{4,3,1,2,0:T(8,128)} %slice_bitcast_fusion), channel_id=1, source_target_pairs={{0,16},{16,0},{1,17},{17,1},{2,18},{18,2},{3,19},{19,3},{4,20},{20... | collective-permute-start | bytes 4718600 | tf_op jit(solution)/shard_map/ppermute | solution.py:14
Sparse Core Ops, SparseCore 0:
  10.2 44.0 all-gather.4
  100.0 70.6 reduce-scatter.1
